TPU v7x, 256 devices: a whole 4x4x8 slice. The times are simulated.
256 devices in a mesh: snap: 8 (over x, core), slab: 32 (over y, z).
Axes of the slice: x: 4, y: 4, z: 8, core: 2. Of those that a mesh axis runs over, the one named last changes fastest.
Arguments:
- velocity: bfloat16 [256, 3, 160, 8, 128], P('snap', None, 'slab'), may hold values from -10 to 10
Outputs:
- modes: bfloat16 [768, 32, 5120], P(None, 'slab', 'snap')
- factor: float32 [768, 768], replicated
All inputs are finite; a program needn't handle non-finite values.
Results may differ from a plain program's by a relative error of at most 0.0004.
The roundings to bfloat16 on the way count: a program that leaves them out, or rounds other values in their place, can miss the bound.
Values may be sent and summed in bfloat16 or wider, within the bound.
No kernel may reach another device: no remote copies, remote signals or barrier semaphores. Data moves between devices by JAX's collectives and lax.ppermute only.
A program may use at most 64 MiB of HBM per device.

v0:
```python
import jax
import jax.numpy as jnp
from jax import lax
from jax.sharding import PartitionSpec as P

stencil_weights = (4.0 / 5.0, -1.0 / 5.0, 4.0 / 105.0, -1.0 / 280.0)


def with_halo(block, sides, width):
    for axis, dim in sides:
        count = lax.axis_size(axis)
        forward = [(i, i + 1) for i in range(count - 1)]
        backward = [(target, source) for source, target in forward]
        low = lax.ppermute(
            lax.slice_in_dim(block, block.shape[dim] - width, None, axis=dim), axis, forward
        )
        high = lax.ppermute(lax.slice_in_dim(block, 0, width, axis=dim), axis, backward)
        block = jnp.concatenate([low, block, high], axis=dim)
    return block


def differ(padded, axis, length):
    total = None
    for offset in range(4):
        step = offset + 1
        ahead = lax.slice_in_dim(padded, 4 + step, 4 + step + length, axis=axis)
        behind = lax.slice_in_dim(padded, 4 - step, 4 - step + length, axis=axis)
        term = stencil_weights[offset] * (ahead - behind)
        total = term if total is None else total + term
    return total


def derive(field, axis):
    widths = [(0, 0)] * field.ndim
    widths[axis] = (4, 4)
    return differ(jnp.pad(field, widths), axis, field.shape[axis])


def reduce_entries(entries):
    share = lax.psum_scatter(entries, ("snap", "slab"), scatter_dimension=0, tiled=True)
    total = lax.all_gather(share, ("snap", "slab"), axis=0, tiled=True)
    return total


def padded_sum(entries):
    summed = reduce_entries(entries)
    return summed


def body(velocity):
    planes = velocity.shape[2]
    extended = with_halo(velocity, (("slab", 2),), 4)
    second_rim = extended[:, 1].astype(jnp.float32)
    third_rim = extended[:, 2].astype(jnp.float32)
    first = velocity[:, 0].astype(jnp.float32)
    second = velocity[:, 1].astype(jnp.float32)
    third = velocity[:, 2].astype(jnp.float32)
    omega_one = derive(third, 2) - derive(second, 3)
    omega_two = derive(first, 3) - differ(third_rim, 1, planes)
    omega_three = differ(second_rim, 1, planes) - derive(first, 2)
    vorticity = jnp.stack([omega_one, omega_two, omega_three], axis=1).astype(jnp.bfloat16)
    local_snaps = vorticity.shape[0]
    flat = vorticity.reshape(local_snaps, 3, -1)
    regrouped = lax.all_to_all(flat, "snap", split_axis=2, concat_axis=0, tiled=True)
    width = regrouped.shape[0] * 3
    matrix = regrouped.reshape(width, -1)
    rows = matrix.shape[1]
    gram = lax.dot_general(
        matrix, matrix, (((1,), (1,)), ((), ())), preferred_element_type=jnp.float32
    )
    total = padded_sum(gram.reshape(-1)).reshape(width, width)
    point_count = rows * lax.axis_size("snap") * lax.axis_size("slab")
    lower = jnp.linalg.cholesky(total / point_count)
    factor = lower.T
    solved = jax.scipy.linalg.solve_triangular(lower, matrix.astype(jnp.float32), lower=True)
    modes = solved.astype(jnp.bfloat16).reshape(width, 1, rows)
    return (modes, factor)


def solution(mesh):
    in_specs = (P("snap", None, "slab", None, None),)
    out_specs = (P(None, "slab", "snap"), P())
    return jax.shard_map(body, mesh=mesh, in_specs=in_specs, out_specs=out_specs, check_vma=False)
```

profile of v0, /device:TPU:1, one launch (start us, length us, event | category | flops | bytes accessed | tf_op | source)
XLA Modules:
  0.0 749.4 jit_solution(7124444804363547871)
XLA Ops:
  8.5 4.4 collective-permute-start
  13.9 15.1 %collective-permute-done = bf16[32,3,4,8,128]{4,3,2,1,0:T(8,128)(2,1)S(1)} collective-permute-done((bf16[32,3,4,8,128]{4,3,2,1,0:T(8,128)(2,1)S(1)}, bf16[32,3,4,8,128]{4,3,2,1,0:T(8,128)(2,1)S(1)}, u32[]{:S(2)}, u32[]{:S(2)}) %collective-permute-start) | collective-permute-done | bytes 786464 | tf_op jit(solution)/shard_map/ppermute | solution.py:14
  32.7 17.3 %collective-permute-done.1 = bf16[32,3,4,8,128]{4,3,2,0,1:T(8,128)(2,1)S(1)} collective-permute-done((bf16[32,3,4,8,128]{4,3,2,0,1:T(8,128)(2,1)S(1)}, bf16[32,3,4,8,128]{4,3,2,0,1:T(8,128)(2,1)S(1)}, u32[]{:S(2)}, u32[]{:S(2)}) %collective-permute-start.1) | collective-permute-done | bytes 786464 | tf_op jit(solution)/shard_map/ppermute | solution.py:17
  51.1 1.6 fusion.22
  52.8 2.3 fusion.29
  55.5 5.0 copy.42
  60.5 6.9 reshape.211
  67.5 20.5 %all_to_all.15 = bf16[8,2,30720]{2,1,0:T(2,128)(2,1)S(1)} all-to-all(bf16[8,2,30720]{2,1,0:T(2,128)(2,1)S(1)} %reshape.211), channel_id=1, replica_groups=mesh['snap'=8,'slab'=32] {'snap'}, dimensions={0} | all-to-all | bytes 1966080 | tf_op jit(solution)/shard_map/all_to_all | solution.py:64
  88.0 5.4 reshape.212
  93.4 5.4 copy.47
  101.6 1.6 reshape.180
  103.5 263.8 %all-reduce.8.cloned.1.call-done = f32[589824]{0:T(1024)} async-done(((f32[589824]{0:T(1024)}), f32[589824]{0:T(1024)}) %all-reduce.8.cloned.1.call-update) | async-done | bytes 2359312
  368.8 1.4 convert_element_type.53
  370.2 106.2 %all-gather.3.cloned.1.call-done = f32[256,1,2304]{2,1,0:T(1,128)} async-done(((f32[1,1,2304]{2,1,0:T(1,128)}), f32[256,1,2304]{2,1,0:T(1,128)}) %all-gather.3.cloned.1.call-update) | async-done | bytes 2359312 | tf_op jit(solution)/shard_map/all_gather | solution.py:41
  476.4 10.2 %multiply_reduce_fusion = f32[256,2304]{1,0:T(8,128)} fusion(f32[256,1,2304]{2,1,0:T(1,128)} %all-gather.3.cloned.1.call-done), kind=kLoop, calls=%fused_computation.20 | loop fusion | flops 589824 | bytes 4718592 | tf_op jit(solution)/shard_map/div | solution.py:73
  486.5 2.5 div.18
  489.0 2.3 copy.45
  491.4 2.0 fusion
  494.7 11.7 %cholesky.165 = f32[128,128]{1,0:T(8,128)S(1)} custom-call(f32[128,128]{1,0:T(8,128)S(1)} %cholesky.424), custom_call_target="Cholesky" | custom-call | tf_op jit(solution)/shard_map/jit(cholesky)/cholesky | solution.py:73
  506.5 9.8 %custom-call.47 = f32[1,128,128]{1,2,0:T(8,128)S(1)} custom-call(f32[1,128,128]{2,1,0:T(8,128)S(1)} %get-tuple-element.55), custom_call_target="InvertDiagBlocksLowerTriangular" | custom-call | tf_op jit(solution)/shard_map/jit(cholesky)/cholesky | solution.py:73
  517.9 1.4 convolution_subtract_fusion.2
  520.0 11.7 %cholesky.188 = f32[128,128]{1,0:T(8,128)S(1)} custom-call(f32[128,128]{1,0:T(8,128)S(1)} %cholesky.428), custom_call_target="Cholesky" | custom-call | tf_op jit(solution)/shard_map/jit(cholesky)/cholesky | solution.py:73
  531.7 9.9 %custom-call.48 = f32[1,128,128]{1,2,0:T(8,128)S(1)} custom-call(f32[1,128,128]{2,1,0:T(8,128)S(1)} %get-tuple-element.52), custom_call_target="InvertDiagBlocksLowerTriangular" | custom-call | tf_op jit(solution)/shard_map/jit(cholesky)/cholesky | solution.py:73
  543.0 1.5 convolution_subtract_fusion.5
  545.3 11.7 %cholesky.354 = f32[128,128]{1,0:T(8,128)S(1)} custom-call(f32[128,128]{1,0:T(8,128)S(1)} %cholesky.433), custom_call_target="Cholesky" | custom-call | tf_op jit(solution)/shard_map/jit(cholesky)/cholesky | solution.py:73
  557.7 9.8 %custom-call.49 = f32[1,128,128]{1,2,0:T(8,128)S(1)} custom-call(f32[1,128,128]{2,1,0:T(8,128)S(1)} %get-tuple-element.49), custom_call_target="InvertDiagBlocksLowerTriangular" | custom-call | tf_op jit(solution)/shard_map/jit(cholesky)/cholesky | solution.py:73
  568.8 1.6 convolution_subtract_fusion.6
  570.9 13.4 %cholesky.373 = f32[128,128]{1,0:T(8,128)} custom-call(f32[128,128]{1,0:T(8,128)} %cholesky.438), custom_call_target="Cholesky" | custom-call | tf_op jit(solution)/shard_map/jit(cholesky)/cholesky | solution.py:73
  584.3 1.5 select_reduce_fusion.2
  586.4 11.3 %custom-call.50 = f32[1,128,128]{1,2,0:T(8,128)} custom-call(f32[1,128,128]{2,1,0:T(8,128)} %get-tuple-element.46), custom_call_target="InvertDiagBlocksLowerTriangular" | custom-call | tf_op jit(solution)/shard_map/jit(cholesky)/cholesky | solution.py:73
  598.8 1.5 convolution_subtract_fusion.7
  600.3 12.3 %cholesky.392 = f32[128,128]{1,0:T(8,128)} custom-call(f32[128,128]{1,0:T(8,128)S(1)} %cholesky.443), custom_call_target="Cholesky" | custom-call | tf_op jit(solution)/shard_map/jit(cholesky)/cholesky | solution.py:73
  614.2 10.4 %custom-call.51 = f32[1,128,128]{1,2,0:T(8,128)} custom-call(f32[1,128,128]{2,1,0:T(8,128)S(1)} %get-tuple-element.43), custom_call_target="InvertDiagBlocksLowerTriangular" | custom-call | tf_op jit(solution)/shard_map/jit(cholesky)/cholesky | solution.py:73
  627.0 11.9 %cholesky.410 = f32[128,128]{1,0:T(8,128)S(1)} custom-call(f32[128,128]{1,0:T(8,128)S(1)} %convolution_subtract_fusion.8), custom_call_target="Cholesky" | custom-call | tf_op jit(solution)/shard_map/jit(cholesky)/cholesky | solution.py:73
  643.8 2.4 fusion.2
  646.3 3.2 copy.46
  649.5 20.4 %while.1 = (s32[]{:T(128)}, f32[768,768]{1,0:T(8,128)}, s32[6,2]{0,1:T(2,128)S(1)}, f32[6,128,128]{2,1,0:T(8,128)}, s32[]{:T(128)}) while((s32[]{:T(128)}, f32[768,768]{1,0:T(8,128)}, s32[6,2]{0,1:T(2,128)S(1)}, f32[6,128,128]{2,1,0:T(8,128)}, s32[]{:T(128)}) %tuple.50), condition=%wide.while_cond, body=%wide.while_body.sunk | while | flops 2 | bytes 132205 | solution.py:75
  650.1 2.8 bitcast_dynamic-update-slice_fusion.7
  653.5 2.8 bitcast_dynamic-update-slice_fusion.7
  656.9 2.8 bitcast_dynamic-update-slice_fusion.7
  660.3 2.8 bitcast_dynamic-update-slice_fusion.7
  663.7 2.8 bitcast_dynamic-update-slice_fusion.7
  667.1 2.7 bitcast_dynamic-update-slice_fusion.7
  669.9 59.8 %custom-call.52 = f32[6,128,128]{1,2,0:T(8,128)S(1)} custom-call(f32[6,128,128]{2,1,0:T(8,128)} %get-tuple-element.9), custom_call_target="InvertDiagBlocksLowerTriangular" | custom-call | tf_op jit(solution)/shard_map/jit(_solve_triangular)/triangular_solve | solution.py:75
  731.8 1.4 convolution_subtract_fusion
  733.7 1.8 convolution_subtract_fusion.4
  736.0 1.9 fusion.11
  738.5 2.2 convolution_subtract_fusion.3
  (87 shorter events, 35.8 us)
Async XLA Ops:
  7.2 22.0 %copy-start.2 = (bf16[32,3,5,8,128]{4,3,2,1,0:T(8,128)(2,1)S(1)}, bf16[32,3,5,8,128]{4,3,2,1,0:T(8,128)(2,1)}, u32[]{:S(2)}) copy-start(bf16[32,3,5,8,128]{4,3,2,1,0:T(8,128)(2,1)} %param.1) | copy-start | bytes 2949124
  7.2 360.1 %all-reduce.8.cloned.1.call-start = ((), (), s32[]{:S(2)}) async-start(), calls=%async_computation.2 | async-start | bytes 4718592
  8.5 20.6 %collective-permute-start = (bf16[32,3,4,8,128]{4,3,2,1,0:T(8,128)(2,1)S(1)}, bf16[32,3,4,8,128]{4,3,2,1,0:T(8,128)(2,1)S(1)}, u32[]{:S(2)}, u32[]{:S(2)}) collective-permute-start(bf16[32,3,4,8,128]{4,3,2,1,0:T(8,128)(2,1)S(1)} %slice.372), channel_id=1, source_target_pairs={{0,1},{1,2},{2,3},{3,4},{4,5},{5,6},{6,7},{7,8},{8,9},{9,10},{10,1... | collective-permute-start | bytes 2359304 | tf_op jit(solution)/shard_map/ppermute | solution.py:14
  29.5 1.6 copy-start.3
  29.5 20.5 %collective-permute-start.1 = (bf16[32,3,4,8,128]{4,3,2,0,1:T(8,128)(2,1)S(1)}, bf16[32,3,4,8,128]{4,3,2,0,1:T(8,128)(2,1)S(1)}, u32[]{:S(2)}, u32[]{:S(2)}) collective-permute-start(bf16[32,3,4,8,128]{4,3,2,0,1:T(8,128)(2,1)S(1)} %slice.429), channel_id=1, source_target_pairs={{1,0},{2,1},{3,2},{4,3},{5,4},{6,5},{7,6},{8,7},{9,8},{10,9},{11,1... | collective-permute-start | bytes 2359304 | tf_op jit(solution)/shard_map/ppermute | solution.py:17
  103.2 373.1 %all-gather.3.cloned.1.call-start = ((), (), s32[]{:S(2)}) async-start(), calls=%async_computation.1 | async-start | bytes 2368512 | tf_op jit(solution)/shard_map/all_gather | solution.py:41
  493.3 1.4 copy-start
  519.3 0.7 copy-start.4
  544.6 0.7 copy-start.5
  646.3 83.8 %copy-start.1 = (f32[768,640]{1,0:T(8,128)S(1)}, f32[768,640]{1,0:T(8,128)}, u32[]{:S(2)}) copy-start(f32[768,640]{1,0:T(8,128)} %convert_element_type.53) | copy-start | bytes 5898244
  741.2 0.9 copy-start.6
Sparse Core Ops, SparseCore 0:
  103.3 263.9 all-reduce.7
  371.4 104.8 all-gather.2
where the time goes:
time: 758 us; the launch traced here: 749 us
  waiting for transfers between devices  402 us (53%)
  other arithmetic  212 us (28%)
  local copies, waits for them, and re-layouts  63.8 us (8%)
  matrix products  25.8 us (3%)
  blocking collectives  20.5 us (3%)
  between operations  18.6 us (2%)
    unnamed x3, waiting for transfers between devices  264 us
    another operation x22, other arithmetic, body(): lower = jnp.linalg.cholesky(total / point_count)  130 us
    all_gather x1, waiting for transfers between devices, reduce_entries(): total = lax.all_gather(share, ('snap', 'slab'), axis=0, tiled=True)  106 us
    another operation x2, other arithmetic, body(): jax.scipy.linalg.solve_triangular(lower, matrix.astype(jnp.float32), lowe...  59.8 us
    unnamed x25, local copies, waits for them, and re-layouts  21.1 us
    all_to_all x1, blocking collectives, body(): lax.all_to_all(flat, 'snap', split_axis=2, concat_axis=0, tiled=True)  20.5 us
    another operation x18, local copies, waits for them, and re-layouts  20.4 us
    ppermute x1, waiting for transfers between devices, with_halo(): lax.ppermute(lax.slice_in_dim(block, 0, width, axis=dim), axis, backward)  17.3 us
  transfers between devices with their start and end apart: 4, of which 4 were waited for; matrix products, arithmetic and copies ran while one was open for 1% of the time, Pallas kernels for 0%

commit v1 on v0

--- a/solution.py
+++ b/solution.py
@@ -38,7 +38,12 @@
 
 def reduce_entries(entries):
     share = lax.psum_scatter(entries, ("snap", "slab"), scatter_dimension=0, tiled=True)
-    total = lax.all_gather(share, ("snap", "slab"), axis=0, tiled=True)
+    total = jnp.concatenate(
+        lax.all_to_all(
+            jnp.stack([share] * lax.axis_size(("snap", "slab"))), ("snap", "slab"), 0, 0
+        ),
+        axis=0,
+    )
     return total
 
 

time: 758 us -> 724 us (0.955)
  waiting for transfers between devices: 402 us -> 355 us
  starting transfers between devices: 5.99 us -> 18.3 us
    all_gather x1 -> x0, waiting for transfers between devices: 106 us -> none  [reduce_entries(): total = lax.all_gather(share, ('snap', 'slab'), axis=0, tiled=True)]
    all_to_all x0 -> x1, waiting for transfers between devices: none -> 58.4 us  [reduce_entries(): lax.all_to_all(jnp.stack([share] * lax.axis_size(('snap', 'slab'))), ('sn...]
    all_to_all x0 -> x1, starting transfers between devices: none -> 12.5 us  [reduce_entries(): lax.all_to_all(jnp.stack([share] * lax.axis_size(('snap', 'slab'))), ('sn...]
    another operation x18 -> x19, local copies, waits for them, and re-layouts: 20.4 us -> 23 us
    unnamed x25 -> x24, local copies, waits for them, and re-layouts: 21.1 us -> 20.5 us
    unnamed x3 -> x2, waiting for transfers between devices: 264 us -> 264 us
where the time goes in v1:
time: 724 us; the launch traced here: 714 us
  waiting for transfers between devices  355 us (49%)
  other arithmetic  210 us (29%)
  local copies, waits for them, and re-layouts  65.8 us (9%)
  matrix products  25.8 us (4%)
  blocking collectives  20.5 us (3%)
  between operations  18.6 us (3%)
  starting transfers between devices  18.3 us (3%)
    unnamed x2, waiting for transfers between devices  264 us
    another operation x22, other arithmetic, body(): lower = jnp.linalg.cholesky(total / point_count)  130 us
    another operation x2, other arithmetic, body(): jax.scipy.linalg.solve_triangular(lower, matrix.astype(jnp.float32), lowe...  59.8 us
    all_to_all x1, waiting for transfers between devices, reduce_entries(): lax.all_to_all(jnp.stack([share] * lax.axis_size(('snap', 'slab'))), ('sn...  58.4 us
    unnamed x24, local copies, waits for them, and re-layouts  20.5 us
    all_to_all x1, blocking collectives, body(): lax.all_to_all(flat, 'snap', split_axis=2, concat_axis=0, tiled=True)  20.5 us
    another operation x18, local copies, waits for them, and re-layouts  20.4 us
    ppermute x1, waiting for transfers between devices, with_halo(): lax.ppermute(lax.slice_in_dim(block, 0, width, axis=dim), axis, backward)  17.3 us
  transfers between devices with their start and end apart: 4, of which 4 were waited for; matrix products, arithmetic and copies ran while one was open for 1% of the time, Pallas kernels for 0%

profile of v1, /device:TPU:1, one launch (start us, length us, event | category | flops | bytes accessed | tf_op | source)
XLA Modules:
  0.0 714.2 jit_solution(7006768474954239122)
XLA Ops:
  8.5 4.4 collective-permute-start
  13.9 15.1 %collective-permute-done = bf16[32,3,4,8,128]{4,3,2,1,0:T(8,128)(2,1)S(1)} collective-permute-done((bf16[32,3,4,8,128]{4,3,2,1,0:T(8,128)(2,1)S(1)}, bf16[32,3,4,8,128]{4,3,2,1,0:T(8,128)(2,1)S(1)}, u32[]{:S(2)}, u32[]{:S(2)}) %collective-permute-start) | collective-permute-done | bytes 786464 | tf_op jit(solution)/shard_map/ppermute | solution.py:14
  32.7 17.3 %collective-permute-done.1 = bf16[32,3,4,8,128]{4,3,2,0,1:T(8,128)(2,1)S(1)} collective-permute-done((bf16[32,3,4,8,128]{4,3,2,0,1:T(8,128)(2,1)S(1)}, bf16[32,3,4,8,128]{4,3,2,0,1:T(8,128)(2,1)S(1)}, u32[]{:S(2)}, u32[]{:S(2)}) %collective-permute-start.1) | collective-permute-done | bytes 786464 | tf_op jit(solution)/shard_map/ppermute | solution.py:17
  51.1 1.6 fusion.22
  52.8 2.3 fusion.29
  55.5 5.0 copy.42
  60.5 6.9 reshape.213
  67.5 20.5 %all_to_all.21 = bf16[8,2,30720]{2,1,0:T(2,128)(2,1)S(1)} all-to-all(bf16[8,2,30720]{2,1,0:T(2,128)(2,1)S(1)} %reshape.213), channel_id=1, replica_groups=mesh['snap'=8,'slab'=32] {'snap'}, dimensions={0} | all-to-all | bytes 1966080 | tf_op jit(solution)/shard_map/all_to_all | solution.py:69
  88.0 5.4 reshape.214
  93.4 5.4 copy.47
  101.6 1.6 reshape.187
  103.2 264.1 %all-reduce.8.cloned.1.call-done = f32[589824]{0:T(1024)} async-done(((f32[589824]{0:T(1024)}), f32[589824]{0:T(1024)}) %all-reduce.8.cloned.1.call-update) | async-done | bytes 2359312
  368.1 2.6 stack.14
  370.7 12.5 %all-to-all-start.1 = ((f32[256,1,2304]{2,1,0:T(1,128)}), f32[256,1,2304]{2,1,0:T(1,128)S(1)}, u32[]{:S(2)}, u32[]{:S(2)}) async-start(f32[256,1,2304]{2,1,0:T(1,128)} %stack.14), calls=%async_computation.1 | async-start | bytes 4718592 | tf_op jit(solution)/shard_map/all_to_all | solution.py:42
  383.3 1.4 convert_element_type.53
  384.7 58.4 %all-to-all-done.1 = f32[256,1,2304]{2,1,0:T(1,128)S(1)} async-done(((f32[256,1,2304]{2,1,0:T(1,128)}), f32[256,1,2304]{2,1,0:T(1,128)S(1)}, u32[]{:S(2)}, u32[]{:S(2)}) %all-to-all-start.1) | async-done | bytes 2359328 | tf_op jit(solution)/shard_map/all_to_all | solution.py:42
  443.1 8.2 %multiply_reduce_fusion = f32[256,2304]{1,0:T(8,128)} fusion(f32[256,1,2304]{2,1,0:T(1,128)S(1)} %all-to-all-done.1), kind=kLoop, calls=%fused_computation.21 | loop fusion | flops 589824 | bytes 4718592 | tf_op jit(solution)/shard_map/div | solution.py:78
  451.3 2.5 div.18
  453.8 2.3 copy.45
  456.1 2.0 fusion
  459.5 11.7 %cholesky.165 = f32[128,128]{1,0:T(8,128)S(1)} custom-call(f32[128,128]{1,0:T(8,128)S(1)} %cholesky.424), custom_call_target="Cholesky" | custom-call | tf_op jit(solution)/shard_map/jit(cholesky)/cholesky | solution.py:78
  471.2 9.8 %custom-call.47 = f32[1,128,128]{1,2,0:T(8,128)S(1)} custom-call(f32[1,128,128]{2,1,0:T(8,128)S(1)} %get-tuple-element.55), custom_call_target="InvertDiagBlocksLowerTriangular" | custom-call | tf_op jit(solution)/shard_map/jit(cholesky)/cholesky | solution.py:78
  484.8 11.7 %cholesky.188 = f32[128,128]{1,0:T(8,128)S(1)} custom-call(f32[128,128]{1,0:T(8,128)S(1)} %cholesky.428), custom_call_target="Cholesky" | custom-call | tf_op jit(solution)/shard_map/jit(cholesky)/cholesky | solution.py:78
  496.5 9.9 %custom-call.48 = f32[1,128,128]{1,2,0:T(8,128)S(1)} custom-call(f32[1,128,128]{2,1,0:T(8,128)S(1)} %get-tuple-element.52), custom_call_target="InvertDiagBlocksLowerTriangular" | custom-call | tf_op jit(solution)/shard_map/jit(cholesky)/cholesky | solution.py:78
  507.8 1.5 convolution_subtract_fusion.5
  510.0 11.7 %cholesky.354 = f32[128,128]{1,0:T(8,128)S(1)} custom-call(f32[128,128]{1,0:T(8,128)S(1)} %cholesky.433), custom_call_target="Cholesky" | custom-call | tf_op jit(solution)/shard_map/jit(cholesky)/cholesky | solution.py:78
  522.5 9.8 %custom-call.49 = f32[1,128,128]{1,2,0:T(8,128)S(1)} custom-call(f32[1,128,128]{2,1,0:T(8,128)S(1)} %get-tuple-element.49), custom_call_target="InvertDiagBlocksLowerTriangular" | custom-call | tf_op jit(solution)/shard_map/jit(cholesky)/cholesky | solution.py:78
  533.5 1.6 convolution_subtract_fusion.6
  535.7 13.4 %cholesky.373 = f32[128,128]{1,0:T(8,128)} custom-call(f32[128,128]{1,0:T(8,128)} %cholesky.438), custom_call_target="Cholesky" | custom-call | tf_op jit(solution)/shard_map/jit(cholesky)/cholesky | solution.py:78
  549.1 1.5 select_reduce_fusion.2
  551.2 11.3 %custom-call.50 = f32[1,128,128]{1,2,0:T(8,128)} custom-call(f32[1,128,128]{2,1,0:T(8,128)} %get-tuple-element.46), custom_call_target="InvertDiagBlocksLowerTriangular" | custom-call | tf_op jit(solution)/shard_map/jit(cholesky)/cholesky | solution.py:78
  563.5 1.5 convolution_subtract_fusion.7
  565.0 12.3 %cholesky.392 = f32[128,128]{1,0:T(8,128)} custom-call(f32[128,128]{1,0:T(8,128)S(1)} %cholesky.443), custom_call_target="Cholesky" | custom-call | tf_op jit(solution)/shard_map/jit(cholesky)/cholesky | solution.py:78
  578.9 10.4 %custom-call.51 = f32[1,128,128]{1,2,0:T(8,128)} custom-call(f32[1,128,128]{2,1,0:T(8,128)S(1)} %get-tuple-element.43), custom_call_target="InvertDiagBlocksLowerTriangular" | custom-call | tf_op jit(solution)/shard_map/jit(cholesky)/cholesky | solution.py:78
  591.7 11.9 %cholesky.410 = f32[128,128]{1,0:T(8,128)S(1)} custom-call(f32[128,128]{1,0:T(8,128)S(1)} %convolution_subtract_fusion.8), custom_call_target="Cholesky" | custom-call | tf_op jit(solution)/shard_map/jit(cholesky)/cholesky | solution.py:78
  608.6 2.4 fusion.2
  611.0 3.2 copy.46
  614.2 20.4 %while.1 = (s32[]{:T(128)}, f32[768,768]{1,0:T(8,128)}, s32[6,2]{0,1:T(2,128)S(1)}, f32[6,128,128]{2,1,0:T(8,128)}, s32[]{:T(128)}) while((s32[]{:T(128)}, f32[768,768]{1,0:T(8,128)}, s32[6,2]{0,1:T(2,128)S(1)}, f32[6,128,128]{2,1,0:T(8,128)}, s32[]{:T(128)}) %tuple.50), condition=%wide.while_cond, body=%wide.while_body.sunk | while | flops 2 | bytes 132205 | solution.py:80
  614.8 2.8 bitcast_dynamic-update-slice_fusion.7
  618.2 2.8 bitcast_dynamic-update-slice_fusion.7
  621.6 2.8 bitcast_dynamic-update-slice_fusion.7
  625.1 2.8 bitcast_dynamic-update-slice_fusion.7
  628.5 2.8 bitcast_dynamic-update-slice_fusion.7
  631.9 2.7 bitcast_dynamic-update-slice_fusion.7
  634.6 59.8 %custom-call.52 = f32[6,128,128]{1,2,0:T(8,128)S(1)} custom-call(f32[6,128,128]{2,1,0:T(8,128)} %get-tuple-element.9), custom_call_target="InvertDiagBlocksLowerTriangular" | custom-call | tf_op jit(solution)/shard_map/jit(_solve_triangular)/triangular_solve | solution.py:80
  698.5 1.8 convolution_subtract_fusion.4
  700.8 1.9 fusion.11
  703.3 2.2 convolution_subtract_fusion.3
  (86 shorter events, 37.8 us)
Async XLA Ops:
  7.2 22.0 %copy-start.2 = (bf16[32,3,5,8,128]{4,3,2,1,0:T(8,128)(2,1)S(1)}, bf16[32,3,5,8,128]{4,3,2,1,0:T(8,128)(2,1)}, u32[]{:S(2)}) copy-start(bf16[32,3,5,8,128]{4,3,2,1,0:T(8,128)(2,1)} %param.1) | copy-start | bytes 2949124
  7.2 360.1 %all-reduce.8.cloned.1.call-start = ((), (), s32[]{:S(2)}) async-start(), calls=%async_computation.2 | async-start | bytes 4718592
  8.5 20.6 %collective-permute-start = (bf16[32,3,4,8,128]{4,3,2,1,0:T(8,128)(2,1)S(1)}, bf16[32,3,4,8,128]{4,3,2,1,0:T(8,128)(2,1)S(1)}, u32[]{:S(2)}, u32[]{:S(2)}) collective-permute-start(bf16[32,3,4,8,128]{4,3,2,1,0:T(8,128)(2,1)S(1)} %slice.372), channel_id=1, source_target_pairs={{0,1},{1,2},{2,3},{3,4},{4,5},{5,6},{6,7},{7,8},{8,9},{9,10},{10,1... | collective-permute-start | bytes 2359304 | tf_op jit(solution)/shard_map/ppermute | solution.py:14
  29.5 1.6 copy-start.3
  29.5 20.5 %collective-permute-start.1 = (bf16[32,3,4,8,128]{4,3,2,0,1:T(8,128)(2,1)S(1)}, bf16[32,3,4,8,128]{4,3,2,0,1:T(8,128)(2,1)S(1)}, u32[]{:S(2)}, u32[]{:S(2)}) collective-permute-start(bf16[32,3,4,8,128]{4,3,2,0,1:T(8,128)(2,1)S(1)} %slice.429), channel_id=1, source_target_pairs={{1,0},{2,1},{3,2},{4,3},{5,4},{6,5},{7,6},{8,7},{9,8},{10,9},{11,1... | collective-permute-start | bytes 2359304 | tf_op jit(solution)/shard_map/ppermute | solution.py:17
  370.7 72.4 %all-to-all-start.1 = ((f32[256,1,2304]{2,1,0:T(1,128)}), f32[256,1,2304]{2,1,0:T(1,128)S(1)}, u32[]{:S(2)}, u32[]{:S(2)}) async-start(f32[256,1,2304]{2,1,0:T(1,128)} %stack.14), calls=%async_computation.1 | async-start | bytes 4718592 | tf_op jit(solution)/shard_map/all_to_all | solution.py:42
  458.1 1.4 copy-start
  484.0 0.7 copy-start.4
  509.3 0.7 copy-start.5
  611.0 83.8 %copy-start.1 = (f32[768,640]{1,0:T(8,128)S(1)}, f32[768,640]{1,0:T(8,128)}, u32[]{:S(2)}) copy-start(f32[768,640]{1,0:T(8,128)} %convert_element_type.53) | copy-start | bytes 5898244
  706.0 0.9 copy-start.6
Sparse Core Ops, SparseCore 0:
  103.3 263.9 all-reduce.7
